TPU v7x, 256 devices: a whole 4x4x8 slice. The times are simulated.
256 devices in a mesh: slab: 64 (over y, z, x_lo), ffn: 4 (over x_hi, core).
Axes of the slice: x: 4 (x_hi: 2, x_lo: 2; x = x_hi * 2 + x_lo), y: 4, z: 8, core: 2. Of those that a mesh axis runs over, the one named last changes fastest.
Arguments:
- tokens: bfloat16 [32768, 512], P('slab'), may hold values from -6 to 6
- gain_attn: float32 [512], replicated, may hold values from 0.1 to 1.9
- w_reduce: bfloat16 [4096, 512], replicated, may hold values from -0.09375 to 0.09375
- gain_keys: float32 [512], replicated, may hold values from 0.1 to 1.9
- w_query: bfloat16 [512, 512], P(None, 'ffn'), may hold values from -1.5 to 1.5
- w_key: bfloat16 [512, 512], P(None, 'ffn'), may hold values from -1.5 to 1.5
- w_value: bfloat16 [512, 512], P(None, 'ffn'), may hold values from -0.25 to 0.25
- w_out: bfloat16 [512, 512], P('ffn'), may hold values from -1.796875 to 1.796875
- gain_ffn: float32 [512], replicated, may hold values from 0.1 to 1.9
- w_up: bfloat16 [512, 2048], P(None, 'ffn'), may hold values from -0.25 to 0.25
- w_depth: float32 [27, 2048], P(None, 'ffn'), may hold values from -1.25 to 1.25
- w_down: bfloat16 [2048, 512], P('ffn'), may hold values from -0.125 to 0.125
- grad_out: bfloat16 [32768, 512], P('slab'), may hold values from -0.0625 to 0.0625
Outputs:
- attended: bfloat16 [32768, 512], P('slab')
- grad_up: float32 [512, 2048], P('slab', 'ffn')
- grad_down: float32 [512, 2048], P('slab', 'ffn')
All inputs are finite; a program needn't handle non-finite values.
Results may differ from a plain program's by a relative error of at most 0.024.
The roundings to bfloat16 on the way count: a program that leaves them out, or rounds other values in their place, can miss the bound.
Values may be sent and summed in bfloat16 or wider, within the bound.
A program may use at most 64 MiB of HBM per device.

v0:
```python
import math
import jax
import jax.numpy as jnp
from jax import lax
from jax.sharding import Mesh
from jax.sharding import PartitionSpec as P

HEAD = 64
GX = 16
GY = 16
CZ = 2
SLAB = ("y", "z", "xl")
FFN = ("xh", "core")
EPSILON = 1e-05
ROPE_BASE = 100.0
ROOT_HALF = 0.7071067811865476
NORMAL_SCALE = 0.3989422804014327


def padded_2(cells, sides, width):
    for axis, dim in sides:
        count = lax.psum(1, axis)
        ends = count - 1
        head = lax.slice_in_dim(cells, 0, width, axis=dim)
        tail = lax.slice_in_dim(cells, cells.shape[dim] - width, cells.shape[dim], axis=dim)
        cells = jnp.concatenate(
            [
                lax.ppermute(tail, axis, [(i, (i + 1) % count) for i in range(ends)]),
                cells,
                lax.ppermute(head, axis, [((i + 1) % count, i) for i in range(ends)]),
            ],
            axis=dim,
        )
    return cells


def layer_norm(values, scale_gain):
    values = values.astype(jnp.float32)
    centered = values - jnp.mean(values, axis=-1, keepdims=True)
    variance = jnp.mean(centered * centered, axis=-1, keepdims=True)
    return centered * lax.rsqrt(variance + EPSILON) * scale_gain


def rope_tables(coord_x, coord_y, coord_z, head_size):
    pair_count = head_size // 2
    position = jnp.arange(pair_count, dtype=jnp.int32)
    axis_pick = position % 3
    per_axis = (pair_count + 2) // 3
    frequency = ROPE_BASE ** (-(position // 3).astype(jnp.float32) / per_axis)
    angles = (
        coord_x[:, None] * (axis_pick == 0)
        + coord_y[:, None] * (axis_pick == 1)
        + coord_z[:, None] * (axis_pick == 2)
    ) * frequency
    return (jnp.cos(angles)[:, None, :], jnp.sin(angles)[:, None, :])


def token_tables(first_plane, planes, head_size):
    position = jnp.arange(planes * GY * GX, dtype=jnp.int32)
    coord_x = (position % GX).astype(jnp.float32)
    coord_y = (position // GX % GY).astype(jnp.float32)
    coord_z = (first_plane + position // (GX * GY)).astype(jnp.float32)
    return rope_tables(coord_x, coord_y, coord_z, head_size)


def key_tables(first_row, row_count, head_size):
    position = first_row + jnp.arange(row_count, dtype=jnp.int32)
    half_x = GX // 2
    half_y = GY // 2
    coord_x = (position % half_x).astype(jnp.float32) * 2.0 + 0.5
    coord_y = (position // half_x % half_y).astype(jnp.float32) * 2.0 + 0.5
    coord_z = (position // (half_x * half_y)).astype(jnp.float32) * 2.0 + 0.5
    return rope_tables(coord_x, coord_y, coord_z, head_size)


def rotate(values, cosine, sine_table):
    half_size = values.shape[-1] // 2
    front_half = values[..., :half_size]
    back_half = values[..., half_size:]
    return jnp.concatenate(
        [
            front_half * cosine - back_half * sine_table,
            back_half * cosine + front_half * sine_table,
        ],
        axis=-1,
    )


def make_patches(normed, planes):
    width = normed.shape[-1]
    cell_grid = normed.reshape(planes // 2, 2, GY // 2, 2, GX // 2, 2, width)
    return cell_grid.transpose(0, 2, 4, 1, 3, 5, 6).reshape(-1, 8 * width)


def depth_conv(padded, weights, planes):
    height = padded.shape[1] - 2
    width_x = padded.shape[2] - 2
    result = jnp.zeros((planes, height, width_x, padded.shape[3]), jnp.float32)
    for offset in range(27):
        shift_z = offset // 9
        shift_y = offset // 3 % 3
        shift_x = offset % 3
        window = padded[
            shift_z : shift_z + planes, shift_y : shift_y + height, shift_x : shift_x + width_x
        ]
        result = result + window.astype(jnp.float32) * weights[offset]
    return result


def attend_piece(state_tuple, queries, key_rows, value_rows):
    row_max, row_sum, weighted = state_tuple
    score_scale = key_rows.shape[-1] ** (-0.5)
    scores = (
        jnp.einsum("qhd,khd->hqk", queries, key_rows, preferred_element_type=jnp.float32)
        * score_scale
    )
    new_max = jnp.maximum(row_max, jnp.max(scores, axis=2))
    rescale = jnp.exp(row_max - new_max)
    expo = jnp.exp(scores - new_max[:, :, None])
    row_sum = row_sum * rescale + jnp.sum(expo, axis=2)
    weighted = weighted * rescale[:, :, None] + jnp.einsum(
        "hqk,khd->hqd", expo.astype(jnp.bfloat16), value_rows, preferred_element_type=jnp.float32
    )
    return (new_max, row_sum, weighted)


def per_device(
    tokens,
    gain_attn,
    w_reduce,
    gain_keys,
    w_query,
    w_key,
    w_value,
    w_out,
    gain_ffn,
    w_up,
    w_depth,
    w_down,
    grad_out,
):
    slab_index = lax.axis_index(SLAB)
    tok_rows = tokens.shape[0]
    heads_dev = w_query.shape[1] // HEAD
    normed = layer_norm(tokens, gain_attn).astype(jnp.bfloat16)
    patches = make_patches(normed, CZ)
    reduced = jnp.dot(patches, w_reduce, preferred_element_type=jnp.float32)
    key_input = layer_norm(reduced, gain_keys).astype(jnp.bfloat16)
    tok_cos, tok_sin = token_tables(slab_index * CZ, CZ, HEAD)
    queries = jnp.dot(normed, w_query, preferred_element_type=jnp.float32).reshape(
        tok_rows, heads_dev, HEAD
    )
    queries = rotate(queries, tok_cos, tok_sin).astype(jnp.bfloat16)
    initial = (
        jnp.full((heads_dev, tok_rows), -1e30, jnp.float32),
        jnp.zeros((heads_dev, tok_rows), jnp.float32),
        jnp.zeros((heads_dev, tok_rows, HEAD), jnp.float32),
    )
    state_tuple = initial
    local_rows = key_input.shape[0]
    own_cos, own_sin = key_tables(slab_index * local_rows, local_rows, HEAD)
    own_keys = jnp.dot(key_input, w_key, preferred_element_type=jnp.float32).reshape(
        local_rows, heads_dev, HEAD
    )
    own_keys = rotate(own_keys, own_cos, own_sin).astype(jnp.bfloat16)
    own_values = jnp.dot(key_input, w_value, preferred_element_type=jnp.float32).astype(
        jnp.bfloat16
    )
    key_width = heads_dev * HEAD
    pieces = jnp.concatenate([own_keys.reshape(local_rows, key_width), own_values], axis=1)
    for axis in ("xl", "z", "y"):
        pieces = lax.all_gather(pieces, axis, axis=0, tiled=True)
    row_count = pieces.shape[0]
    block_rows = math.gcd(row_count, 1024)
    block_count = row_count // block_rows
    blocks = pieces.reshape(block_count, block_rows, pieces.shape[1])

    def one_block(state_inner, rows_in):
        key_block = rows_in[:, :key_width].reshape(block_rows, heads_dev, HEAD)
        value_block = rows_in[:, key_width:].reshape(block_rows, heads_dev, HEAD)
        return (attend_piece(state_inner, queries, key_block, value_block), None)

    state_tuple, _ = lax.scan(one_block, state_tuple, blocks)
    row_max, row_sum, weighted = state_tuple
    heads_out = (
        (weighted / row_sum[:, :, None])
        .transpose(1, 0, 2)
        .reshape(tok_rows, heads_dev * HEAD)
        .astype(jnp.bfloat16)
    )
    partial_value = jnp.dot(heads_out, w_out, preferred_element_type=jnp.float32)
    head_total = lax.psum(partial_value.astype(jnp.bfloat16), FFN).astype(jnp.float32)
    attended = head_total.astype(jnp.bfloat16)
    residual = tokens.astype(jnp.float32) + head_total
    normed_ffn = layer_norm(residual, gain_ffn).astype(jnp.bfloat16)
    channels = w_up.shape[1]
    pre = (
        jnp.dot(normed_ffn, w_up, preferred_element_type=jnp.float32)
        .astype(jnp.bfloat16)
        .reshape(CZ, GY, GX, channels)
    )
    pre_wide = padded_2(pre, ((SLAB, 0),), 1)
    pre_pad = jnp.pad(pre_wide, ((0, 0), (1, 1), (1, 1), (0, 0)))
    mixed = depth_conv(pre_pad, w_depth, CZ).reshape(tok_rows, channels)
    normal_cdf = 0.5 * (1.0 + lax.erf(mixed * ROOT_HALF))
    normal_pdf = jnp.exp(-0.5 * mixed * mixed) * NORMAL_SCALE
    activated = (mixed * normal_cdf).astype(jnp.bfloat16)
    grad_act = jnp.einsum("td,cd->tc", grad_out, w_down, preferred_element_type=jnp.float32)
    grad_mixed = (
        (grad_act * (normal_cdf + mixed * normal_pdf))
        .astype(jnp.bfloat16)
        .reshape(CZ, GY, GX, channels)
    )
    grad_wide = padded_2(grad_mixed, ((SLAB, 0),), 1)
    grad_pad = jnp.pad(grad_wide, ((0, 0), (1, 1), (1, 1), (0, 0)))
    grad_pre = (
        depth_conv(grad_pad, w_depth[::-1], CZ).astype(jnp.bfloat16).reshape(tok_rows, channels)
    )
    up_full = jnp.einsum("td,tc->dc", normed_ffn, grad_pre, preferred_element_type=jnp.float32)
    down_full = jnp.einsum("td,tc->dc", grad_out, activated, preferred_element_type=jnp.float32)
    grads = jnp.concatenate([up_full, down_full], axis=1)
    sizes = [lax.psum(1, axis) for axis in SLAB]
    grads = grads.reshape(sizes + [-1, grads.shape[1]])
    grads = grads.transpose(1, 0, 2, 3, 4).reshape(-1, grads.shape[-1])
    for axis in ("z", "y", "xl"):
        grads = lax.psum_scatter(grads, axis, scatter_dimension=0, tiled=True)
    return (attended, grads[:, :channels], grads[:, channels:])


def solution(mesh):
    mesh = Mesh(mesh.devices.reshape(4, 8, 2, 2, 2), SLAB + FFN)
    in_specs = (
        P(SLAB, None),
        P(),
        P(),
        P(),
        P(None, FFN),
        P(None, FFN),
        P(None, FFN),
        P(FFN, None),
        P(),
        P(None, FFN),
        P(None, FFN),
        P(FFN, None),
        P(SLAB, None),
    )
    out_specs = (P(SLAB, None), P(SLAB, FFN), P(SLAB, FFN))
    return jax.shard_map(
        per_device, mesh=mesh, in_specs=in_specs, out_specs=out_specs, check_vma=False
    )
```

profile of v0, /device:TPU:1, one launch (start us, length us, event | category | flops | bytes accessed | tf_op | source)
XLA Modules:
  0.0 315.7 jit_solution(17436997218391451417)
XLA Ops:
  8.9 1.3 fusion.25
  12.5 3.2 %fusion.75 = (f32[64]{0:T(128)S(1)}, f32[64,512]{1,0:T(8,128)S(1)}) fusion(bf16[64,4096]{1,0:T(8,128)(2,1)S(1)} %reshape.621, bf16[4096,512]{1,0:T(8,128)(2,1)} %param.17), kind=kOutput, calls=%fused_computation.155 | convolution fusion | flops 268468160 | bytes 4849920 | tf_op jit(solution)/shard_map/dot_general | solution.py:147
  16.9 4.0 %all_gather.9 = bf16[128,256]{1,0:T(8,128)(2,1)S(1)} all-gather(bf16[64,256]{1,0:T(8,128)(2,1)S(1)} %pad_maximum_fusion.7), channel_id=1, replica_groups=mesh['y'=4,'z'=8,'xl'=2,'xh'=2,'core'=2] {'xl'}, dimensions={0}, use_global_device_ids=true | all-gather | bytes 98304 | tf_op jit(solution)/shard_map/all_gather | solution.py:172
  20.9 25.7 %all_gather.10 = bf16[1024,256]{1,0:T(8,128)(2,1)} all-gather(bf16[128,256]{1,0:T(8,128)(2,1)S(1)} %all_gather.9), channel_id=1, replica_groups=mesh['y'=4,'z'=8,'xl'=2,'xh'=2,'core'=2] {'z'}, dimensions={0}, use_global_device_ids=true | all-gather | bytes 589824 | tf_op jit(solution)/shard_map/all_gather | solution.py:172
  47.4 39.0 %all-gather.2.cloned.1.call-done = bf16[4096,256]{1,0:T(8,128)(2,1)} async-done(((bf16[1024,256]{1,0:T(8,128)(2,1)}), bf16[4096,256]{1,0:T(8,128)(2,1)}) %all-gather.2.cloned.1.call-update) | async-done | bytes 2097168 | tf_op jit(solution)/shard_map/all_gather | solution.py:172
  86.4 33.6 %while.15 = (s32[]{:T(128)}, f32[2,512]{1,0:T(2,128)S(1)}, f32[2,512]{1,0:T(2,128)S(1)}, f32[2,512,64]{1,2,0:T(8,128)S(1)}, bf16[4,1024,256]{2,1,0:T(8,128)(2,1)...) while((s32[]{:T(128)}, f32[2,512]{1,0:T(2,128)S(1)}, f32[2,512]{1,0:T(2,128)S(1)}, ...), condition=%wide.region_7.8_spmd.clone, body=%wide.region_4.7_spmd.clone.sunk | while | flops 277025792 | bytes 33751168 | solution.py:183
  87.8 2.7 bitcast_reduce_fusion.2
  90.5 3.0 fusion.109
  96.2 2.7 bitcast_reduce_fusion.2
  98.9 3.0 fusion.109
  104.6 2.7 bitcast_reduce_fusion.2
  107.3 3.0 fusion.109
  112.9 2.7 bitcast_reduce_fusion.2
  115.7 3.0 fusion.109
  121.3 47.8 %all-reduce.4.cloned.1.call-done = bf16[512,512]{1,0:T(8,128)(2,1)} async-done(((bf16[512,512]{1,0:T(8,128)(2,1)}), bf16[512,512]{1,0:T(8,128)(2,1)}) %all-reduce.4.cloned.1.call-update) | async-done | bytes 524304 | tf_op jit(solution)/shard_map/psum | solution.py:192
  170.4 1.3 multiply_reduce_fusion
  171.7 1.6 convolution_convert_fusion
  173.3 2.2 collective-permute-start
  176.9 4.1 %collective-permute-done = bf16[1,16,16,512]{3,2,1,0:T(8,128)(2,1)S(1)} collective-permute-done((bf16[1,16,16,512]{3,2,1,0:T(8,128)(2,1)S(1)}, bf16[1,16,16,512]{3,2,1,0:T(8,128)(2,1)S(1)}, u32[]{:S(2)}, u32[]{:S(2)}) %collective-permute-start) | collective-permute-done | bytes 262176 | tf_op jit(solution)/shard_map/ppermute | solution.py:28
  181.1 10.8 %collective-permute-done.1 = bf16[1,16,16,512]{3,2,1,0:T(8,128)(2,1)S(1)} collective-permute-done((bf16[1,16,16,512]{3,2,1,0:T(8,128)(2,1)S(1)}, bf16[1,16,16,512]{3,2,1,0:T(8,128)(2,1)S(1)}, u32[]{:S(2)}, u32[]{:S(2)}) %collective-permute-start.1) | collective-permute-done | bytes 262176 | tf_op jit(solution)/shard_map/ppermute | solution.py:30
  192.7 3.8 %multiply_add_fusion = f32[2,16,16,512]{3,2,1,0:T(8,128)S(1)} fusion(bf16[2,16,16,512]{3,2,1,0:T(8,128)(2,1)S(1)} %bitcast.119, bf16[4,18,18,512]{3,2,1,0:T(8,128)(2,1)S(1)} %fusion.21, bf16[1,16,16,512]{3,2,1,0:T(8,128)(2,1)S(1)} %collective-permute-done.1, bf16[1,16,16,512]{3,2,1,0:T(8,128)(2,1)S(1)} %collective-permute-done, f32[512]{0:T(512)S(1)} %bitcast.141, ...), kind=kLoop, calls=%fused_computation.59 | loop fusion | flops 21495808 | bytes 14735360 | tf_op jit(solution)/shard_map/add | solution.py:106
  197.4 1.3 collective-permute-start.2
  198.7 1.5 collective-permute-start.3
  200.6 8.7 %collective-permute-done.2 = bf16[1,16,16,512]{3,2,1,0:T(8,128)(2,1)S(1)} collective-permute-done((bf16[1,16,16,512]{3,2,1,0:T(8,128)(2,1)S(1)}, bf16[1,16,16,512]{3,2,1,0:T(8,128)(2,1)S(1)}, u32[]{:S(2)}, u32[]{:S(2)}) %collective-permute-start.2) | collective-permute-done | bytes 262176 | tf_op jit(solution)/shard_map/ppermute | solution.py:28
  209.3 4.0 %collective-permute-done.3 = bf16[1,16,16,512]{3,2,1,0:T(8,128)(2,1)S(1)} collective-permute-done((bf16[1,16,16,512]{3,2,1,0:T(8,128)(2,1)S(1)}, bf16[1,16,16,512]{3,2,1,0:T(8,128)(2,1)S(1)}, u32[]{:S(2)}, u32[]{:S(2)}) %collective-permute-start.3) | collective-permute-done | bytes 262176 | tf_op jit(solution)/shard_map/ppermute | solution.py:30
  214.1 3.8 %add_convert_fusion = bf16[2,16,16,512]{3,2,1,0:T(8,128)(2,1)S(1)} fusion(bf16[2,16,16,512]{3,2,1,0:T(8,128)(2,1)S(1)} %bitcast.115, bf16[4,18,18,512]{3,2,1,0:T(8,128)(2,1)S(1)} %select_maximum_fusion, bf16[1,16,16,512]{3,2,1,0:T(8,128)(2,1)S(1)} %collective-permute-done.3, bf16[1,16,16,512]{3,2,1,0:T(8,128)(2,1)S(1)} %collective-permute-done.2, ...), kind=kLoop, calls=%fused_computation.58 | loop fusion | flops 21757952 | bytes 14211072 | tf_op jit(solution)/shard_map/convert_element_type | solution.py:217
  218.9 1.8 copy.33
  220.7 3.2 %copy.34 = f32[8,4,2,8,1024]{4,3,2,1,0:T(8,128)} copy(f32[8,4,2,8,1024]{4,3,2,0,1:T(8,128)} %bitcast.117) | data formatting | bytes 4194304 | tf_op jit(solution)/shard_map/transpose | solution.py:224
  223.9 37.7 %reduce-scatter.4.cloned.1.call-done = f32[64,1024]{1,0:T(8,128)} async-done(((f32[512,1024]{1,0:T(8,128)}), f32[64,1024]{1,0:T(8,128)}) %reduce-scatter.4.cloned.1.call-update) | async-done | bytes 262160 | tf_op jit(solution)/shard_map/reduce_scatter | solution.py:226
  261.7 26.5 %reduce-scatter.6.cloned.1.call-done = f32[16,1024]{1,0:T(8,128)} async-done(((f32[64,1024]{1,0:T(8,128)}), f32[16,1024]{1,0:T(8,128)}) %reduce-scatter.6.cloned.1.call-update) | async-done | bytes 65552 | tf_op jit(solution)/shard_map/reduce_scatter | solution.py:226
  288.2 18.9 %reduce-scatter.8.cloned.1.call-done = f32[8,1024]{1,0:T(8,128)} async-done(((f32[16,1024]{1,0:T(8,128)}), f32[8,1024]{1,0:T(8,128)}) %reduce-scatter.8.cloned.1.call-update) | async-done | bytes 32784 | tf_op jit(solution)/shard_map/reduce_scatter | solution.py:226
  307.1 1.3 fusion.74
  (122 shorter events, 24.8 us)
Async XLA Ops:
  7.2 189.6 %copy-start = (bf16[512,512]{1,0:T(8,128)(2,1)S(1)}, bf16[512,512]{1,0:T(8,128)(2,1)}, u32[]{:S(2)}) copy-start(bf16[512,512]{1,0:T(8,128)(2,1)} %param.27) | copy-start | bytes 1572868
  7.2 79.2 %all-gather.2.cloned.1.call-start = ((), (), s32[]{:S(2)}) async-start(), calls=%async_computation.3 | async-start | bytes 2621440 | tf_op jit(solution)/shard_map/all_gather | solution.py:172
  11.7 4.2 %copy-start.6 = (bf16[512,128]{1,0:T(8,128)(2,1)S(1)}, bf16[512,128]{1,0:T(8,128)(2,1)}, u32[]{:S(2)}) copy-start(bf16[512,128]{1,0:T(8,128)(2,1)} %param.20) | copy-start | bytes 393220
  11.7 4.2 %copy-start.10 = (f32[512]{0:T(512)S(1)}, f32[512]{0:T(512)}, u32[]{:S(2)}) copy-start(f32[512]{0:T(512)} %param.18) | copy-start | bytes 6148
  12.1 4.5 %copy-start.7 = (bf16[512,128]{1,0:T(8,128)(2,1)S(1)}, bf16[512,128]{1,0:T(8,128)(2,1)}, u32[]{:S(2)}) copy-start(bf16[512,128]{1,0:T(8,128)(2,1)} %param.21) | copy-start | bytes 393220
  12.5 34.5 %copy-start.5 = (bf16[512,128]{1,0:T(8,128)(2,1)S(1)}, bf16[512,128]{1,0:T(8,128)(2,1)}, u32[]{:S(2)}) copy-start(bf16[512,128]{1,0:T(8,128)(2,1)} %param.19) | copy-start | bytes 393220
  46.6 122.5 %all-reduce.4.cloned.1.call-start = ((), (), s32[]{:S(2)}) async-start(), calls=%async_computation.4 | async-start | bytes 1048576 | tf_op jit(solution)/shard_map/psum | solution.py:192
  86.4 33.7 %copy-start.8 = (bf16[128,512]{1,0:T(8,128)(2,1)S(1)}, bf16[128,512]{1,0:T(8,128)(2,1)}, u32[]{:S(2)}) copy-start(bf16[128,512]{1,0:T(8,128)(2,1)} %param.22) | copy-start | bytes 393220
  86.4 82.7 %copy-start.2 = (bf16[512,512]{1,0:T(8,128)(2,1)S(1)}, bf16[512,512]{1,0:T(8,128)(2,1)}, u32[]{:S(2)}) copy-start(bf16[512,512]{1,0:T(8,128)(2,1)} %param.15) | copy-start | bytes 1572868
  90.5 3.4 %copy-start.1 = (f32[2,1024,512]{2,1,0:T(8,128)S(1)}, f32[2,1024,512]{2,1,0:T(8,128)}, u32[]{:S(2)}) copy-start(f32[2,1024,512]{2,1,0:T(8,128)} %get-tuple-element.197) | copy-start | bytes 12582916 | tf_op jit(solution)/shard_map/while
  98.9 3.4 %copy-start.1 = (f32[2,1024,512]{2,1,0:T(8,128)S(1)}, f32[2,1024,512]{2,1,0:T(8,128)}, u32[]{:S(2)}) copy-start(f32[2,1024,512]{2,1,0:T(8,128)} %get-tuple-element.197) | copy-start | bytes 12582916 | tf_op jit(solution)/shard_map/while
  107.3 3.4 %copy-start.1 = (f32[2,1024,512]{2,1,0:T(8,128)S(1)}, f32[2,1024,512]{2,1,0:T(8,128)}, u32[]{:S(2)}) copy-start(f32[2,1024,512]{2,1,0:T(8,128)} %get-tuple-element.197) | copy-start | bytes 12582916 | tf_op jit(solution)/shard_map/while
  115.6 3.4 %copy-start.1 = (f32[2,1024,512]{2,1,0:T(8,128)S(1)}, f32[2,1024,512]{2,1,0:T(8,128)}, u32[]{:S(2)}) copy-start(f32[2,1024,512]{2,1,0:T(8,128)} %get-tuple-element.197) | copy-start | bytes 12582916 | tf_op jit(solution)/shard_map/while
  120.0 51.7 %copy-start.11 = (bf16[512,512]{1,0:T(8,128)(2,1)S(1)}, bf16[512,512]{1,0:T(8,128)(2,1)}, u32[]{:S(2)}) copy-start(bf16[512,512]{1,0:T(8,128)(2,1)} %param.24) | copy-start | bytes 1572868
  120.0 51.7 %copy-start.12 = (f32[512]{0:T(512)S(1)}, f32[512]{0:T(512)}, u32[]{:S(2)}) copy-start(f32[512]{0:T(512)} %param.23) | copy-start | bytes 6148
  120.1 56.8 %copy-start.9 = (f32[27,512]{1,0:T(8,128)S(1)}, f32[27,512]{1,0:T(8,128)}, u32[]{:S(2)}) copy-start(f32[27,512]{1,0:T(8,128)} %param.25) | copy-start | bytes 165892
  121.2 140.4 %reduce-scatter.4.cloned.1.call-start = ((), (), s32[]{:S(2)}) async-start(), calls=%async_computation.5 | async-start | bytes 2359296 | tf_op jit(solution)/shard_map/reduce_scatter | solution.py:226
  173.3 7.7 %collective-permute-start = (bf16[1,16,16,512]{3,2,1,0:T(8,128)(2,1)S(1)}, bf16[1,16,16,512]{3,2,1,0:T(8,128)(2,1)S(1)}, u32[]{:S(2)}, u32[]{:S(2)}) collective-permute-start(bf16[1,16,16,512]{3,2,1,0:T(8,128)(2,1)S(1)} %bitcast.126), channel_id=1, source_target_pairs={{0,4},{4,8},{8,12},{12,16},{16,20},{20,24},{24,28},{28,32},{32,36}... | collective-permute-start | bytes 786440 | tf_op jit(solution)/shard_map/ppermute | solution.py:28
  175.6 16.3 %collective-permute-start.1 = (bf16[1,16,16,512]{3,2,1,0:T(8,128)(2,1)S(1)}, bf16[1,16,16,512]{3,2,1,0:T(8,128)(2,1)S(1)}, u32[]{:S(2)}, u32[]{:S(2)}) collective-permute-start(bf16[1,16,16,512]{3,2,1,0:T(8,128)(2,1)S(1)} %bitcast.125), channel_id=1, source_target_pairs={{4,0},{8,4},{12,8},{16,12},{20,16},{24,20},{28,24},{32,28},{36,32}... | collective-permute-start | bytes 786440 | tf_op jit(solution)/shard_map/ppermute | solution.py:30
  192.7 4.1 %copy-start.4 = (bf16[512,512]{1,0:T(8,128)(2,1)S(1)}, bf16[512,512]{1,0:T(8,128)(2,1)}, u32[]{:S(2)}) copy-start(bf16[512,512]{1,0:T(8,128)(2,1)} %param.26) | copy-start | bytes 1572868
  197.4 11.9 %collective-permute-start.2 = (bf16[1,16,16,512]{3,2,1,0:T(8,128)(2,1)S(1)}, bf16[1,16,16,512]{3,2,1,0:T(8,128)(2,1)S(1)}, u32[]{:S(2)}, u32[]{:S(2)}) collective-permute-start(bf16[1,16,16,512]{3,2,1,0:T(8,128)(2,1)S(1)} %bitcast.128), channel_id=1, source_target_pairs={{0,4},{4,8},{8,12},{12,16},{16,20},{20,24},{24,28},{28,32},{32,36}... | collective-permute-start | bytes 786440 | tf_op jit(solution)/shard_map/ppermute | solution.py:28
  198.7 14.6 %collective-permute-start.3 = (bf16[1,16,16,512]{3,2,1,0:T(8,128)(2,1)S(1)}, bf16[1,16,16,512]{3,2,1,0:T(8,128)(2,1)S(1)}, u32[]{:S(2)}, u32[]{:S(2)}) collective-permute-start(bf16[1,16,16,512]{3,2,1,0:T(8,128)(2,1)S(1)} %bitcast.127), channel_id=1, source_target_pairs={{4,0},{8,4},{12,8},{16,12},{20,16},{24,20},{28,24},{32,28},{36,32}... | collective-permute-start | bytes 786440 | tf_op jit(solution)/shard_map/ppermute | solution.py:30
  214.1 3.9 %copy-start.3 = (bf16[512,512]{1,0:T(8,128)(2,1)S(1)}, bf16[512,512]{1,0:T(8,128)(2,1)}, u32[]{:S(2)}) copy-start(bf16[512,512]{1,0:T(8,128)(2,1)} %all-reduce.4.cloned.1.call-done) | copy-start | bytes 1572868
  223.9 64.3 %reduce-scatter.6.cloned.1.call-start = ((), (), s32[]{:S(2)}) async-start(), calls=%async_computation.6 | async-start | bytes 327680 | tf_op jit(solution)/shard_map/reduce_scatter | solution.py:226
  261.7 45.4 %reduce-scatter.8.cloned.1.call-start = ((), (), s32[]{:S(2)}) async-start(), calls=%async_computation.7 | async-start | bytes 98304 | tf_op jit(solution)/shard_map/reduce_scatter | solution.py:226
Sparse Core Ops, SparseCore 0:
  46.7 39.6 all-gather.1
  121.3 47.7 all-reduce.3
  224.0 37.5 reduce-scatter.3
  264.0 24.1 reduce-scatter.5
  290.6 16.4 reduce-scatter.7
where the time goes:
time: 316 us
  waiting for transfers between devices  198 us (63%)
  blocking collectives  29.7 us (9%)
  other arithmetic  29.5 us (9%)
  matrix products  22.5 us (7%)
  local copies, waits for them, and re-layouts  15.5 us (5%)
  between operations  14.3 us (5%)
  starting transfers between devices  6.48 us (2%)
    reduce_scatter x3, waiting for transfers between devices, per_device(): grads = lax.psum_scatter(grads, axis, scatter_dimension=0, tiled=True)  83 us
    psum x1, waiting for transfers between devices, per_device(): lax.psum(partial_value.astype(jnp.bfloat16), FFN).astype(jnp.float32)  47.8 us
    all_gather x1, waiting for transfers between devices, per_device(): pieces = lax.all_gather(pieces, axis, axis=0, tiled=True)  39 us
    all_gather x2, blocking collectives, per_device(): pieces = lax.all_gather(pieces, axis, axis=0, tiled=True)  29.7 us
    ppermute x2, waiting for transfers between devices, padded_2(): lax.ppermute(head, axis, [((i + 1) % count, i) for i in range(ends)])  14.8 us
    ppermute x2, waiting for transfers between devices, padded_2(): lax.ppermute(tail, axis, [(i, (i + 1) % count) for i in range(ends)])  12.8 us
    reduce_sum x4, other arithmetic, attend_piece(): row_sum = row_sum * rescale + jnp.sum(expo, axis=2)  12.1 us
    dot_general x4, matrix products, attend_piece(): jnp.einsum('qhd,khd->hqk', queries, key_rows, preferred_element_type=jnp....  10.8 us
  transfers between devices with their start and end apart: 9, of which 9 were waited for; matrix products, arithmetic and copies ran while one was open for 0% of the time, Pallas kernels for 0%

commit v1 on v0

--- a/solution.py
+++ b/solution.py
@@ -189,7 +189,9 @@
         .astype(jnp.bfloat16)
     )
     partial_value = jnp.dot(heads_out, w_out, preferred_element_type=jnp.float32)
-    head_total = lax.psum(partial_value.astype(jnp.bfloat16), FFN).astype(jnp.float32)
+    head_total = jnp.sum(lax.all_gather(partial_value.astype(jnp.bfloat16), FFN), axis=0).astype(
+        jnp.float32
+    )
     attended = head_total.astype(jnp.bfloat16)
     residual = tokens.astype(jnp.float32) + head_total
     normed_ffn = layer_norm(residual, gain_ffn).astype(jnp.bfloat16)

time: 316 us -> 296 us (0.937)
  waiting for transfers between devices: 198 us -> 179 us
    psum x1 -> x0, waiting for transfers between devices: 47.8 us -> none  [per_device(): lax.psum(partial_value.astype(jnp.bfloat16), FFN).astype(jnp.float32)]
    all_gather x0 -> x1, waiting for transfers between devices: none -> 29.7 us  [per_device(): lax.all_gather(partial_value.astype(jnp.bfloat16), FFN)]
where the time goes in v1:
time: 296 us
  waiting for transfers between devices  179 us (60%)
  blocking collectives  29.7 us (10%)
  other arithmetic  29.6 us (10%)
  matrix products  21.5 us (7%)
  local copies, waits for them, and re-layouts  14.7 us (5%)
  between operations  14.3 us (5%)
  starting transfers between devices  6.48 us (2%)
    reduce_scatter x3, waiting for transfers between devices, per_device(): grads = lax.psum_scatter(grads, axis, scatter_dimension=0, tiled=True)  83 us
    all_gather x1, waiting for transfers between devices, per_device(): pieces = lax.all_gather(pieces, axis, axis=0, tiled=True)  39 us
    all_gather x1, waiting for transfers between devices, per_device(): lax.all_gather(partial_value.astype(jnp.bfloat16), FFN)  29.7 us
    all_gather x2, blocking collectives, per_device(): pieces = lax.all_gather(pieces, axis, axis=0, tiled=True)  29.7 us
    ppermute x2, waiting for transfers between devices, padded_2(): lax.ppermute(head, axis, [((i + 1) % count, i) for i in range(ends)])  14.9 us
    ppermute x2, waiting for transfers between devices, padded_2(): lax.ppermute(tail, axis, [(i, (i + 1) % count) for i in range(ends)])  12.7 us
    reduce_sum x4, other arithmetic, attend_piece(): row_sum = row_sum * rescale + jnp.sum(expo, axis=2)  12.1 us
    dot_general x4, matrix products, attend_piece(): jnp.einsum('qhd,khd->hqk', queries, key_rows, preferred_element_type=jnp....  10.8 us
  transfers between devices with their start and end apart: 9, of which 9 were waited for; matrix products, arithmetic and copies ran while one was open for 0% of the time, Pallas kernels for 0%

profile of v1, /device:TPU:1, one launch (start us, length us, event | category | flops | bytes accessed | tf_op | source)
XLA Modules:
  0.0 295.8 jit_solution(15401518026993502075)
XLA Ops:
  8.9 1.3 fusion.25
  12.5 3.2 %fusion.75 = (f32[64]{0:T(128)S(1)}, f32[64,512]{1,0:T(8,128)S(1)}) fusion(bf16[64,4096]{1,0:T(8,128)(2,1)S(1)} %reshape.621, bf16[4096,512]{1,0:T(8,128)(2,1)} %param.17), kind=kOutput, calls=%fused_computation.155 | convolution fusion | flops 268468160 | bytes 4849920 | tf_op jit(solution)/shard_map/dot_general | solution.py:147
  16.9 4.0 %all_gather.15 = bf16[128,256]{1,0:T(8,128)(2,1)S(1)} all-gather(bf16[64,256]{1,0:T(8,128)(2,1)S(1)} %pad_maximum_fusion.7), channel_id=1, replica_groups=mesh['y'=4,'z'=8,'xl'=2,'xh'=2,'core'=2] {'xl'}, dimensions={0}, use_global_device_ids=true | all-gather | bytes 98304 | tf_op jit(solution)/shard_map/all_gather | solution.py:172
  20.9 25.7 %all_gather.16 = bf16[1024,256]{1,0:T(8,128)(2,1)} all-gather(bf16[128,256]{1,0:T(8,128)(2,1)S(1)} %all_gather.15), channel_id=1, replica_groups=mesh['y'=4,'z'=8,'xl'=2,'xh'=2,'core'=2] {'z'}, dimensions={0}, use_global_device_ids=true | all-gather | bytes 589824 | tf_op jit(solution)/shard_map/all_gather | solution.py:172
  47.4 39.0 %all-gather.4.cloned.1.call-done = bf16[4096,256]{1,0:T(8,128)(2,1)} async-done(((bf16[1024,256]{1,0:T(8,128)(2,1)}), bf16[4096,256]{1,0:T(8,128)(2,1)}) %all-gather.4.cloned.1.call-update) | async-done | bytes 2097168 | tf_op jit(solution)/shard_map/all_gather | solution.py:172
  86.4 33.6 %while.15 = (s32[]{:T(128)}, f32[2,512]{1,0:T(2,128)S(1)}, f32[2,512]{1,0:T(2,128)S(1)}, f32[2,512,64]{1,2,0:T(8,128)S(1)}, bf16[4,1024,256]{2,1,0:T(8,128)(2,1)...) while((s32[]{:T(128)}, f32[2,512]{1,0:T(2,128)S(1)}, f32[2,512]{1,0:T(2,128)S(1)}, ...), condition=%wide.region_7.8_spmd.clone, body=%wide.region_4.7_spmd.clone.sunk | while | flops 277025792 | bytes 33751168 | solution.py:183
  87.7 2.7 bitcast_reduce_fusion.2
  90.5 3.0 %fusion.109 = f32[2,512]{1,0:T(2,128)S(1)} fusion(f32[2,1024,512]{2,1,0:T(8,128)} %get-tuple-element.197, f32[2,512]{1,0:T(2,128)S(1)} %fusion.108), kind=kLoop, calls=%fused_computation.4.clone.1 | loop fusion | flops 3144704 | bytes 4202496 | tf_op jit(solution)/shard_map/while/body/eval_jaxpr/reduce_sum | solution.py:120
  96.1 2.7 bitcast_reduce_fusion.2
  98.8 3.0 %fusion.109 = f32[2,512]{1,0:T(2,128)S(1)} fusion(f32[2,1024,512]{2,1,0:T(8,128)} %get-tuple-element.197, f32[2,512]{1,0:T(2,128)S(1)} %fusion.108), kind=kLoop, calls=%fused_computation.4.clone.1 | loop fusion | flops 3144704 | bytes 4202496 | tf_op jit(solution)/shard_map/while/body/eval_jaxpr/reduce_sum | solution.py:120
  104.5 2.7 bitcast_reduce_fusion.2
  107.2 3.0 %fusion.109 = f32[2,512]{1,0:T(2,128)S(1)} fusion(f32[2,1024,512]{2,1,0:T(8,128)} %get-tuple-element.197, f32[2,512]{1,0:T(2,128)S(1)} %fusion.108), kind=kLoop, calls=%fused_computation.4.clone.1 | loop fusion | flops 3144704 | bytes 4202496 | tf_op jit(solution)/shard_map/while/body/eval_jaxpr/reduce_sum | solution.py:120
  112.9 2.7 bitcast_reduce_fusion.2
  115.6 3.0 %fusion.109 = f32[2,512]{1,0:T(2,128)S(1)} fusion(f32[2,1024,512]{2,1,0:T(8,128)} %get-tuple-element.197, f32[2,512]{1,0:T(2,128)S(1)} %fusion.108), kind=kLoop, calls=%fused_computation.4.clone.1 | loop fusion | flops 3144704 | bytes 4202496 | tf_op jit(solution)/shard_map/while/body/eval_jaxpr/reduce_sum | solution.py:120
  121.2 29.7 %all-gather.6.cloned.1.call-done = bf16[2048,512]{1,0:T(8,128)(2,1)} async-done(((bf16[512,512]{1,0:T(8,128)(2,1)}), bf16[2048,512]{1,0:T(8,128)(2,1)}) %all-gather.6.cloned.1.call-update) | async-done | bytes 2097168 | tf_op jit(solution)/shard_map/all_gather | solution.py:192
  150.9 2.2 reduce_sum.79
  154.3 2.2 collective-permute-start
  156.5 1.3 collective-permute-start.1
  157.9 4.0 %collective-permute-done = bf16[1,16,16,512]{3,2,1,0:T(8,128)(2,1)S(1)} collective-permute-done((bf16[1,16,16,512]{3,2,1,0:T(8,128)(2,1)S(1)}, bf16[1,16,16,512]{3,2,1,0:T(8,128)(2,1)S(1)}, u32[]{:S(2)}, u32[]{:S(2)}) %collective-permute-start) | collective-permute-done | bytes 262176 | tf_op jit(solution)/shard_map/ppermute | solution.py:28
  161.9 10.9 %collective-permute-done.1 = bf16[1,16,16,512]{3,2,1,0:T(8,128)(2,1)S(1)} collective-permute-done((bf16[1,16,16,512]{3,2,1,0:T(8,128)(2,1)S(1)}, bf16[1,16,16,512]{3,2,1,0:T(8,128)(2,1)S(1)}, u32[]{:S(2)}, u32[]{:S(2)}) %collective-permute-start.1) | collective-permute-done | bytes 262176 | tf_op jit(solution)/shard_map/ppermute | solution.py:30
  173.6 3.8 %multiply_add_fusion = f32[2,16,16,512]{3,2,1,0:T(8,128)S(1)} fusion(bf16[2,16,16,512]{3,2,1,0:T(8,128)(2,1)S(1)} %bitcast.120, bf16[4,18,18,512]{3,2,1,0:T(8,128)(2,1)S(1)} %fusion.21, bf16[1,16,16,512]{3,2,1,0:T(8,128)(2,1)S(1)} %collective-permute-done.1, bf16[1,16,16,512]{3,2,1,0:T(8,128)(2,1)S(1)} %collective-permute-done, f32[512]{0:T(512)S(1)} %bitcast.143, ...), kind=kLoop, calls=%fused_computation.59 | loop fusion | flops 21495808 | bytes 14735360 | tf_op jit(solution)/shard_map/add | solution.py:106
  178.3 1.3 collective-permute-start.2
  179.6 1.5 collective-permute-start.3
  181.6 8.7 %collective-permute-done.2 = bf16[1,16,16,512]{3,2,1,0:T(8,128)(2,1)S(1)} collective-permute-done((bf16[1,16,16,512]{3,2,1,0:T(8,128)(2,1)S(1)}, bf16[1,16,16,512]{3,2,1,0:T(8,128)(2,1)S(1)}, u32[]{:S(2)}, u32[]{:S(2)}) %collective-permute-start.2) | collective-permute-done | bytes 262176 | tf_op jit(solution)/shard_map/ppermute | solution.py:28
  190.2 4.0 %collective-permute-done.3 = bf16[1,16,16,512]{3,2,1,0:T(8,128)(2,1)S(1)} collective-permute-done((bf16[1,16,16,512]{3,2,1,0:T(8,128)(2,1)S(1)}, bf16[1,16,16,512]{3,2,1,0:T(8,128)(2,1)S(1)}, u32[]{:S(2)}, u32[]{:S(2)}) %collective-permute-start.3) | collective-permute-done | bytes 262176 | tf_op jit(solution)/shard_map/ppermute | solution.py:30
  195.0 3.8 %add_convert_fusion = bf16[2,16,16,512]{3,2,1,0:T(8,128)(2,1)S(1)} fusion(bf16[2,16,16,512]{3,2,1,0:T(8,128)(2,1)S(1)} %bitcast.116, bf16[4,18,18,512]{3,2,1,0:T(8,128)(2,1)S(1)} %select_maximum_fusion, bf16[1,16,16,512]{3,2,1,0:T(8,128)(2,1)S(1)} %collective-permute-done.3, bf16[1,16,16,512]{3,2,1,0:T(8,128)(2,1)S(1)} %collective-permute-done.2, ...), kind=kLoop, calls=%fused_computation.58 | loop fusion | flops 21757952 | bytes 14211072 | tf_op jit(solution)/shard_map/convert_element_type | solution.py:219
  199.8 1.8 copy.33
  201.6 3.2 %copy.34 = f32[8,4,2,8,1024]{4,3,2,1,0:T(8,128)} copy(f32[8,4,2,8,1024]{4,3,2,0,1:T(8,128)} %bitcast.118) | data formatting | bytes 4194304 | tf_op jit(solution)/shard_map/transpose | solution.py:226
  204.8 37.7 %reduce-scatter.4.cloned.1.call-done = f32[64,1024]{1,0:T(8,128)} async-done(((f32[512,1024]{1,0:T(8,128)}), f32[64,1024]{1,0:T(8,128)}) %reduce-scatter.4.cloned.1.call-update) | async-done | bytes 262160 | tf_op jit(solution)/shard_map/reduce_scatter | solution.py:228
  242.6 26.5 %reduce-scatter.6.cloned.1.call-done = f32[16,1024]{1,0:T(8,128)} async-done(((f32[64,1024]{1,0:T(8,128)}), f32[16,1024]{1,0:T(8,128)}) %reduce-scatter.6.cloned.1.call-update) | async-done | bytes 65552 | tf_op jit(solution)/shard_map/reduce_scatter | solution.py:228
  269.1 18.8 %reduce-scatter.8.cloned.1.call-done = f32[8,1024]{1,0:T(8,128)} async-done(((f32[16,1024]{1,0:T(8,128)}), f32[8,1024]{1,0:T(8,128)}) %reduce-scatter.8.cloned.1.call-update) | async-done | bytes 32784 | tf_op jit(solution)/shard_map/reduce_scatter | solution.py:228
  288.0 1.3 fusion.74
  (122 shorter events, 22.5 us)
Async XLA Ops:
  7.2 170.5 %copy-start = (bf16[512,512]{1,0:T(8,128)(2,1)S(1)}, bf16[512,512]{1,0:T(8,128)(2,1)}, u32[]{:S(2)}) copy-start(bf16[512,512]{1,0:T(8,128)(2,1)} %param.27) | copy-start | bytes 1572868
  7.2 79.2 %all-gather.4.cloned.1.call-start = ((), (), s32[]{:S(2)}) async-start(), calls=%async_computation.3 | async-start | bytes 2621440 | tf_op jit(solution)/shard_map/all_gather | solution.py:172
  11.7 4.2 %copy-start.6 = (bf16[512,128]{1,0:T(8,128)(2,1)S(1)}, bf16[512,128]{1,0:T(8,128)(2,1)}, u32[]{:S(2)}) copy-start(bf16[512,128]{1,0:T(8,128)(2,1)} %param.20) | copy-start | bytes 393220
  11.7 4.2 %copy-start.10 = (f32[512]{0:T(512)S(1)}, f32[512]{0:T(512)}, u32[]{:S(2)}) copy-start(f32[512]{0:T(512)} %param.18) | copy-start | bytes 6148
  12.1 4.5 %copy-start.7 = (bf16[512,128]{1,0:T(8,128)(2,1)S(1)}, bf16[512,128]{1,0:T(8,128)(2,1)}, u32[]{:S(2)}) copy-start(bf16[512,128]{1,0:T(8,128)(2,1)} %param.21) | copy-start | bytes 393220
  12.5 34.5 %copy-start.5 = (bf16[512,128]{1,0:T(8,128)(2,1)S(1)}, bf16[512,128]{1,0:T(8,128)(2,1)}, u32[]{:S(2)}) copy-start(bf16[512,128]{1,0:T(8,128)(2,1)} %param.19) | copy-start | bytes 393220
  46.6 104.4 %all-gather.6.cloned.1.call-start = ((), (), s32[]{:S(2)}) async-start(), calls=%async_computation.7 | async-start | bytes 2621440 | tf_op jit(solution)/shard_map/all_gather | solution.py:192
  86.4 33.7 %copy-start.8 = (bf16[128,512]{1,0:T(8,128)(2,1)S(1)}, bf16[128,512]{1,0:T(8,128)(2,1)}, u32[]{:S(2)}) copy-start(bf16[128,512]{1,0:T(8,128)(2,1)} %param.22) | copy-start | bytes 393220
  90.4 3.4 %copy-start.1 = (f32[2,1024,512]{2,1,0:T(8,128)S(1)}, f32[2,1024,512]{2,1,0:T(8,128)}, u32[]{:S(2)}) copy-start(f32[2,1024,512]{2,1,0:T(8,128)} %get-tuple-element.197) | copy-start | bytes 12582916 | tf_op jit(solution)/shard_map/while
  98.8 3.4 %copy-start.1 = (f32[2,1024,512]{2,1,0:T(8,128)S(1)}, f32[2,1024,512]{2,1,0:T(8,128)}, u32[]{:S(2)}) copy-start(f32[2,1024,512]{2,1,0:T(8,128)} %get-tuple-element.197) | copy-start | bytes 12582916 | tf_op jit(solution)/shard_map/while
  107.2 3.4 %copy-start.1 = (f32[2,1024,512]{2,1,0:T(8,128)S(1)}, f32[2,1024,512]{2,1,0:T(8,128)}, u32[]{:S(2)}) copy-start(f32[2,1024,512]{2,1,0:T(8,128)} %get-tuple-element.197) | copy-start | bytes 12582916 | tf_op jit(solution)/shard_map/while
  115.6 3.4 %copy-start.1 = (f32[2,1024,512]{2,1,0:T(8,128)S(1)}, f32[2,1024,512]{2,1,0:T(8,128)}, u32[]{:S(2)}) copy-start(f32[2,1024,512]{2,1,0:T(8,128)} %get-tuple-element.197) | copy-start | bytes 12582916 | tf_op jit(solution)/shard_map/while
  120.0 33.2 %copy-start.2 = (bf16[512,512]{1,0:T(8,128)(2,1)S(1)}, bf16[512,512]{1,0:T(8,128)(2,1)}, u32[]{:S(2)}) copy-start(bf16[512,512]{1,0:T(8,128)(2,1)} %param.15) | copy-start | bytes 1572868
  120.0 33.7 %copy-start.11 = (bf16[512,512]{1,0:T(8,128)(2,1)S(1)}, bf16[512,512]{1,0:T(8,128)(2,1)}, u32[]{:S(2)}) copy-start(bf16[512,512]{1,0:T(8,128)(2,1)} %param.24) | copy-start | bytes 1572868
  120.0 33.7 %copy-start.12 = (f32[512]{0:T(512)S(1)}, f32[512]{0:T(512)}, u32[]{:S(2)}) copy-start(f32[512]{0:T(512)} %param.23) | copy-start | bytes 6148
  121.2 121.4 %reduce-scatter.4.cloned.1.call-start = ((), (), s32[]{:S(2)}) async-start(), calls=%async_computation.4 | async-start | bytes 2359296 | tf_op jit(solution)/shard_map/reduce_scatter | solution.py:228
  153.1 45.7 %copy-start.3 = (bf16[512,512]{1,0:T(8,128)(2,1)}, bf16[512,512]{1,0:T(8,128)(2,1)S(1)}, u32[]{:S(2)}) copy-start(bf16[512,512]{1,0:T(8,128)(2,1)S(1)} %reduce_sum.79) | copy-start | bytes 1572868
  153.1 4.7 %copy-start.9 = (f32[27,512]{1,0:T(8,128)S(1)}, f32[27,512]{1,0:T(8,128)}, u32[]{:S(2)}) copy-start(f32[27,512]{1,0:T(8,128)} %param.25) | copy-start | bytes 165892
  154.3 7.6 %collective-permute-start = (bf16[1,16,16,512]{3,2,1,0:T(8,128)(2,1)S(1)}, bf16[1,16,16,512]{3,2,1,0:T(8,128)(2,1)S(1)}, u32[]{:S(2)}, u32[]{:S(2)}) collective-permute-start(bf16[1,16,16,512]{3,2,1,0:T(8,128)(2,1)S(1)} %bitcast.128), channel_id=1, source_target_pairs={{0,4},{4,8},{8,12},{12,16},{16,20},{20,24},{24,28},{28,32},{32,36}... | collective-permute-start | bytes 786440 | tf_op jit(solution)/shard_map/ppermute | solution.py:28
  156.5 16.3 %collective-permute-start.1 = (bf16[1,16,16,512]{3,2,1,0:T(8,128)(2,1)S(1)}, bf16[1,16,16,512]{3,2,1,0:T(8,128)(2,1)S(1)}, u32[]{:S(2)}, u32[]{:S(2)}) collective-permute-start(bf16[1,16,16,512]{3,2,1,0:T(8,128)(2,1)S(1)} %bitcast.127), channel_id=1, source_target_pairs={{4,0},{8,4},{12,8},{16,12},{20,16},{24,20},{28,24},{32,28},{36,32}... | collective-permute-start | bytes 786440 | tf_op jit(solution)/shard_map/ppermute | solution.py:30
  173.6 4.1 %copy-start.4 = (bf16[512,512]{1,0:T(8,128)(2,1)S(1)}, bf16[512,512]{1,0:T(8,128)(2,1)}, u32[]{:S(2)}) copy-start(bf16[512,512]{1,0:T(8,128)(2,1)} %param.26) | copy-start | bytes 1572868
  178.3 11.9 %collective-permute-start.2 = (bf16[1,16,16,512]{3,2,1,0:T(8,128)(2,1)S(1)}, bf16[1,16,16,512]{3,2,1,0:T(8,128)(2,1)S(1)}, u32[]{:S(2)}, u32[]{:S(2)}) collective-permute-start(bf16[1,16,16,512]{3,2,1,0:T(8,128)(2,1)S(1)} %bitcast.130), channel_id=1, source_target_pairs={{0,4},{4,8},{8,12},{12,16},{16,20},{20,24},{24,28},{28,32},{32,36}... | collective-permute-start | bytes 786440 | tf_op jit(solution)/shard_map/ppermute | solution.py:28
  179.6 14.6 %collective-permute-start.3 = (bf16[1,16,16,512]{3,2,1,0:T(8,128)(2,1)S(1)}, bf16[1,16,16,512]{3,2,1,0:T(8,128)(2,1)S(1)}, u32[]{:S(2)}, u32[]{:S(2)}) collective-permute-start(bf16[1,16,16,512]{3,2,1,0:T(8,128)(2,1)S(1)} %bitcast.129), channel_id=1, source_target_pairs={{4,0},{8,4},{12,8},{16,12},{20,16},{24,20},{28,24},{32,28},{36,32}... | collective-permute-start | bytes 786440 | tf_op jit(solution)/shard_map/ppermute | solution.py:30
  204.8 64.3 %reduce-scatter.6.cloned.1.call-start = ((), (), s32[]{:S(2)}) async-start(), calls=%async_computation.5 | async-start | bytes 327680 | tf_op jit(solution)/shard_map/reduce_scatter | solution.py:228
  242.6 45.4 %reduce-scatter.8.cloned.1.call-start = ((), (), s32[]{:S(2)}) async-start(), calls=%async_computation.6 | async-start | bytes 98304 | tf_op jit(solution)/shard_map/reduce_scatter | solution.py:228
Sparse Core Ops, SparseCore 0:
  46.7 39.6 all-gather.3
  121.3 29.5 all-gather.5
  204.9 37.6 reduce-scatter.3
  244.9 24.1 reduce-scatter.5
  271.5 16.3 reduce-scatter.7
